TPU v7x, 32 devices: a whole 2x2x4 slice. The times are simulated.
32 devices in a mesh: fsdp: 4 (over x, core), ctx: 2 (over y), tp: 4 (over z).
Axes of the slice: x: 2, y: 2, z: 4, core: 2. Of those that a mesh axis runs over, the one named last changes fastest.
Arguments:
- inputs: bfloat16 [2048, 8, 768], P('ctx', 'fsdp'), may hold values from -6 to 6
- thoughts: bfloat16 [6, 8, 768], P(None, 'fsdp'), may hold values from -6 to 6
- positions: int32 [6, 8], P(None, 'fsdp'), may hold values from 0 to 2047, as said below
- lengths: int32 [8, 3], P('fsdp'), may hold values from 1 to 1024, 2048 in all within a row
- w_qkv: bfloat16 [3, 768, 768], P(None, 'fsdp', 'tp'), may hold values from -0.21875 to 0.21875
- w_out: bfloat16 [768, 768], P('tp', 'fsdp'), may hold values from -3.5 to 3.5
- w_fc: bfloat16 [768, 3072], P('fsdp', 'tp'), may hold values from -0.21875 to 0.21875
- w_proj: bfloat16 [3072, 768], P('tp', 'fsdp'), may hold values from -0.109375 to 0.109375
- norm_gains: bfloat16 [2, 768], P(None, 'fsdp'), may hold values from 0.099609375 to 1.8984375
- norm_biases: bfloat16 [2, 768], P(None, 'fsdp'), may hold values from -0.14941406 to 0.14941406
- out_grad: bfloat16 [2048, 8, 768], P('ctx', 'fsdp'), may hold values from -6 to 6
Outputs:
- output: bfloat16 [2048, 8, 768], P('ctx', 'fsdp')
- d_inputs: float32 [2048, 8, 768], P('ctx', 'fsdp')
- d_thoughts: float32 [6, 8, 768], P(None, 'fsdp')
- d_w_qkv: float32 [3, 768, 768], P(None, 'fsdp', 'tp')
- d_w_out: float32 [768, 768], P('tp', 'fsdp')
- d_w_fc: float32 [768, 3072], P('fsdp', 'tp')
- d_w_proj: float32 [3072, 768], P('tp', 'fsdp')
- d_norm_gains: float32 [2, 768], P(None, 'fsdp')
- d_bias_first: float32 [768], P('fsdp')
- d_bias_second: float32 [768], P('fsdp')
Inputs may be any that keep to these rules, and one draw needn't show every extreme that they name: Each entry is a position of its sequence; the 6 positions of one sequence are distinct.
All inputs are finite; a program needn't handle non-finite values.
Results may differ from a plain program's by a relative error of at most 0.017.
Values may be sent and summed in bfloat16 or wider, within the bound.
A program may use at most 192 MiB of HBM per device.

v0:
```python
import functools

import jax
import jax.numpy as jnp
from jax import lax
from jax.experimental import pallas as pl
from jax.experimental.pallas import tpu as pltpu
from jax.sharding import PartitionSpec as P

HEAD_DIM = 64
DOC_MOST = 1024
EPSILON = 1e-05
MASKED = -1e30


def dot(a, b, dims=((1,), (0,))):
    return lax.dot_general(a, b, (dims, ((), ())), preferred_element_type=jnp.float32)


def hat_rows(values):
    centre = jnp.mean(values, axis=-1, keepdims=True)
    shifted = values - centre
    spread = jnp.mean(shifted * shifted, axis=-1, keepdims=True)
    inv = lax.rsqrt(spread + EPSILON)
    return shifted * inv, inv


def norm_back(hat, inv, gain, grad):
    eg = grad * gain
    return inv * (
        eg
        - jnp.mean(eg, axis=-1, keepdims=True)
        - hat * jnp.mean(eg * hat, axis=-1, keepdims=True)
    )


MESH = pl.DeviceIdType.MESH
VMEM_LIMIT = 62 << 20


def column(index, size=HEAD_DIM):
    return slice(index * size, (index + 1) * size)


def turn(value):
    return value.astype(jnp.float32).T.astype(jnp.bfloat16)


def turn_back(value):
    return value.T.astype(jnp.bfloat16)


def front_kernel(
    sizes, block,
    start_ref, low_ref, wq_ref, wo_ref, wf_ref, wp_ref, par_ref,
    att_ref, q_ref, kv_ref, prev_ref, out_t_ref, log_ref, normed_ref, wl_ref, ow_ref, fc_ref, pj_ref, params_ref,
    start_s, normed_s, wl_s, wo_s, par_s, q_s, kv_s, prev_s, qt_s, ko_s, vto_s, kp_s, vtp_s, m_s, l_s, att_s,
    in_sem, out_sem, w_loc, z_sem, z_rec, s_sem, s_rec, x_sem, x_rec, r_sem, r_rec,
    kv_sem, kv_rec, at_sem, at_rec, at_loc,
):
    F, C, T = sizes
    f, c, t = lax.axis_index("fsdp"), lax.axis_index("ctx"), lax.axis_index("tp")
    S, rows, width = start_ref.shape
    hw = q_ref.shape[2]
    heads = hw // HEAD_DIM
    own_rows = rows // T
    far = prev_ref.shape[1] // rows if C > 1 else 0
    shard = wq_ref.shape[1]
    hidden = wf_ref.shape[1]
    bf, f32 = jnp.bfloat16, jnp.float32
    sib, across = f ^ 1, f ^ 2

    def remote(src, dst, send, recv, **where):
        return pltpu.make_async_remote_copy(
            src_ref=src, dst_ref=dst, send_sem=send, recv_sem=recv, device_id=where, device_id_type=MESH
        )

    start_in = pltpu.make_async_copy(start_ref, start_s, in_sem.at[0])
    start_in.start()

    barrier = pltpu.get_barrier_semaphore()
    peers = 0
    for d in range(1, F):
        pl.semaphore_signal(barrier, inc=1, device_id={"fsdp": f ^ d}, device_id_type=MESH)
        peers += 1
    for d in range(1, T):
        pl.semaphore_signal(barrier, inc=1, device_id={"tp": lax.rem(t + d, T)}, device_id_type=MESH)
        peers += 1
    for d in range(1, C):
        pl.semaphore_signal(barrier, inc=1, device_id={"ctx": lax.rem(c + d, C)}, device_id_type=MESH)
        peers += 1
    pl.semaphore_wait(barrier, peers)

    pending = []

    def go(copy):
        copy.start()
        pending.append(copy)
        return copy

    def at_shard(ff):
        return pl.ds(pl.multiple_of(ff * shard, shard), shard)

    def at_hidden(tt):
        return pl.ds(pl.multiple_of(tt * hidden, hidden), hidden)

    def block_at(a, tt, ff):
        if a == 0:
            return par_s.at[ff]
        if a == 1:
            return wl_s.at[:, at_shard(ff), :]
        if a == 2:
            return wo_s.at[tt, ff]
        return (fc_ref if a == 3 else pj_ref).at[at_shard(ff), at_hidden(tt)]

    sources = (par_ref, wq_ref, wo_ref, wf_ref, wp_ref)

    def origin(p):
        return t if p == 0 else (t - (p + 1) // 2 if p % 2 else t + p // 2)

    def has(p):
        return t >= (p + 1) // 2 if p % 2 else t + p // 2 <= T - 1

    def spread_chip(a, p):
        src = sources[a] if p == 0 else block_at(a, origin(p), f)
        dst = block_at(a, origin(p), f)
        remote(src, dst, x_sem.at[a, p], x_rec.at[a, p], fsdp=across).start()
        remote(src, dst, s_sem.at[a, p], s_rec.at[a, p], fsdp=sib).start()

    def along(a, p, way):
        src = sources[a] if p == 0 else block_at(a, origin(p), f)
        q = p + 2 if p else 1 + way
        return remote(
            src, block_at(a, origin(p), f), z_sem.at[a, p, way], z_rec.at[a, q], tp=t + 1 if way == 0 else t - 1
        )

    def line_start(a):
        @pl.when(t < T - 1)
        def _():
            along(a, 0, 0).start()

        @pl.when(t > 0)
        def _():
            along(a, 0, 1).start()

        spread_chip(a, 0)

    def line_step(a, k):
        for way, p in ((0, 2 * k - 1), (1, 2 * k)):
            on = t < T - 1 if way == 0 else t > 0

            @pl.when(has(p) & on)
            def _():
                here = block_at(a, origin(p), f)
                remote(here, here, z_sem.at[a, p, way], z_rec.at[a, p], tp=t).wait_recv()
                along(a, p, way).start()

            @pl.when(has(p) & jnp.logical_not(on))
            def _():
                here = block_at(a, origin(p), f)
                remote(here, here, z_sem.at[a, p, way], z_rec.at[a, p], tp=t).wait_recv()

            @pl.when(has(p))
            def _():
                spread_chip(a, p)

    def relay(a, p):
        here = block_at(a, origin(p), across)
        remote(here, here, x_sem.at[a, p], x_rec.at[a, p], fsdp=f).wait_recv()
        remote(here, here, r_sem.at[a, p], r_rec.at[a, p], fsdp=sib).start()

    def take_chip(a, p):
        for ff, rec in ((sib, s_rec), (sib ^ 2, r_rec)):
            here = block_at(a, origin(p), ff)
            remote(here, here, s_sem.at[a, p], rec.at[a, p], fsdp=f).wait_recv()

    def every(what, a, ps):
        for p in ps:
            if p == 0:
                what(a, 0)
            else:
                @pl.when(has(p))
                def _():
                    what(a, p)

    def drain(a):
        last = 1 if a < 2 else 2 * T - 1

        def chip(a, p):
            src = sources[a]
            for sem in (x_sem, s_sem, r_sem):
                remote(src, src, sem.at[a, p], x_rec.at[a, p], fsdp=f).wait_send()

        every(chip, a, range(last))
        if a >= 2:
            for p in range(2 * T - 1):
                for way in range(2):
                    if p and p % 2 != 1 - way:
                        continue
                    on = t < T - 1 if way == 0 else t > 0

                    @pl.when((on & has(p)) if p else on)
                    def _():
                        remote(sources[a], sources[a], z_sem.at[a, p, way], z_rec.at[a, p], tp=t).wait_send()

    keeps = []
    for a in range(5):
        keep = pltpu.make_async_copy(sources[a], block_at(a, t, f), w_loc.at[a])
        keep.start()
        keeps.append(keep)
    spread_chip(0, 0)
    spread_chip(1, 0)
    for a in (2, 3, 4):
        line_start(a)

    relay(0, 0)
    take_chip(0, 0)
    keeps[0].wait()
    params = jnp.concatenate([par_s[ff] for ff in range(F)], axis=1)
    params_ref[...] = params
    start_in.wait()
    per_seq = rows // block

    def norm_one(index, _):
        s = index // per_seq
        here = pl.ds(pl.multiple_of(lax.rem(index, per_seq) * block, block), block)
        hat, _ = hat_rows(start_s[s, here, :].astype(f32))
        normed_s[s, here, :] = (hat * params_ref[0:1, :] + params_ref[2:3, :]).astype(bf)
        return 0

    lax.fori_loop(0, S * per_seq, norm_one, 0)
    normed_out = pltpu.make_async_copy(normed_s, normed_ref, out_sem.at[0])
    normed_out.start()

    relay(1, 0)
    take_chip(1, 0)
    keeps[1].wait()

    def kv_one(s, _):
        def one(index, _):
            here = pl.ds(pl.multiple_of(index * block, block), block)
            rows_in = normed_s[s, here, :]
            k = dot(rows_in, wl_s[1]).astype(bf)
            v = dot(rows_in, wl_s[2]).astype(bf)
            kv_s[s, here, :] = jnp.concatenate([k, v], axis=1)
            v_t = turn(v)
            for h in range(heads):
                ko_s[s, h, here, :] = k[:, column(h)]
                vto_s[s, h, :, here] = v_t[column(h)]
            return 0

        lax.fori_loop(0, per_seq, one, 0)
        return 0

    def kv_copy(s, d):
        return remote(
            kv_s.at[s], prev_s.at[s, pl.ds((far - d) * rows, rows), :],
            kv_sem.at[d, s], kv_rec.at[d, s], ctx=lax.rem(c + d, C),
        )

    for s in range(S):
        kv_one(s, 0)
        for d in range(1, far + 1):
            @pl.when(c + d < C)
            def _():
                kv_copy(s, d).start()

    def q_one(index, _):
        s = index // per_seq
        here = pl.ds(pl.multiple_of(lax.rem(index, per_seq) * block, block), block)
        q = dot(normed_s[s, here, :], wl_s[0]).astype(bf)
        q_s[s, here, :] = q
        q_t = turn(q.astype(f32) * 0.125)
        for h in range(heads):
            qt_s[s, h, :, here] = q_t[column(h)]
        return 0

    lax.fori_loop(0, S * per_seq, q_one, 0)
    outs = [
        pltpu.make_async_copy(q_s, q_ref, out_sem.at[1]),
        pltpu.make_async_copy(kv_s, kv_ref, out_sem.at[2]),
        pltpu.make_async_copy(wl_s, wl_ref, out_sem.at[4]),
    ]
    for copy in outs:
        copy.start()

    def own_part(s):
        def one(h, _):
            spot, line = pl.ds(pl.multiple_of(h * HEAD_DIM, HEAD_DIM), HEAD_DIM), pl.ds(h, 1)
            for i in range(per_seq):
                span = column(i, block)
                low = low_ref[s, :, span] - far * rows
                top = i * block + lax.broadcasted_iota(jnp.int32, (1, block), 1)
                first = max(0, i * block - (DOC_MOST - 1)) // block * block
                many = (i + 1) * block - first
                place = first + lax.broadcasted_iota(jnp.int32, (many, 1), 0)
                scores = dot(ko_s[s, h, first : first + many, :], qt_s[s, h, :, span])
                scores = jnp.where((place >= low) & (place <= top), scores, MASKED)
                m = jnp.max(scores, axis=0, keepdims=True)
                p = jnp.exp(scores - m)
                m_s[s, line, span] = m
                l_s[s, line, span] = jnp.sum(p, axis=0, keepdims=True)
                out_t_ref[s, spot, span] = dot(vto_s[s, h, :, first : first + many], p.astype(bf))
            return 0

        lax.fori_loop(0, heads, one, 0)

    def far_part(s):
        for h in range(heads):
            kp_s[h] = prev_s[s, :, column(h)]
            vtp_s[h] = turn(prev_s[s, :, column(heads + h)])

        def one(h, _):
            spot, line = pl.ds(pl.multiple_of(h * HEAD_DIM, HEAD_DIM), HEAD_DIM), pl.ds(h, 1)
            for i in range(per_seq):
                span = column(i, block)
                first = max(0, far * rows + i * block - (DOC_MOST - 1)) // block * block
                if first >= far * rows:
                    continue
                many = far * rows - first
                place = first + lax.broadcasted_iota(jnp.int32, (many, 1), 0)
                scores = dot(kp_s[h, first : first + many, :], qt_s[s, h, :, span])
                scores = jnp.where(place >= low_ref[s, :, span], scores, MASKED)
                old = m_s[s, line, span]
                m = jnp.maximum(old, jnp.max(scores, axis=0, keepdims=True))
                p = jnp.exp(scores - m)
                alpha = jnp.exp(old - m)
                m_s[s, line, span] = m
                l_s[s, line, span] = alpha * l_s[s, line, span] + jnp.sum(p, axis=0, keepdims=True)
                out_t_ref[s, spot, span] = alpha * out_t_ref[s, spot, span] + dot(
                    vtp_s[h, :, first : first + many], p.astype(bf)
                )
            return 0

        lax.fori_loop(0, heads, one, 0)

    def finish_part(s):
        for h in range(heads):
            out_t_ref[s, column(h), :] = out_t_ref[s, column(h), :] / l_s[s, h : h + 1, :]
            log_ref[s, h : h + 1, :] = m_s[s, h : h + 1, :] + jnp.log(l_s[s, h : h + 1, :])
        for tt in range(T):
            att_s[tt, s] = out_t_ref[s, :, column(tt, own_rows)].astype(bf)

    every_p = range(2 * T - 1)
    for a in (2, 3):
        line_step(a, 1)

    def own_loop(s, _):
        own_part(s)
        return 0

    lax.fori_loop(0, 1, own_loop, 0)
    line_step(2, 2)
    line_step(4, 1)
    line_step(3, 2)
    lax.fori_loop(1, S, own_loop, 0)
    for k in range(3, T):
        line_step(2, k)
    every(relay, 2, every_p)

    def wait_far(s):
        for d in range(1, far + 1):
            @pl.when(c >= d)
            def _():
                kv_copy(s, d).wait_recv()

            @pl.when(c < d)
            def _():
                prev_s[s, (far - d) * rows : (far - d + 1) * rows, :] = jnp.zeros((rows, 2 * hw), bf)

    at = [[None] * S for _ in range(T)]
    for s in range(S):
        if far:
            wait_far(s)

            @pl.when(c > 0)
            def _():
                far_part(s)
        finish_part(s)
        for d in range(1, T):
            peer = lax.rem(t + d, T)
            at[d][s] = go(
                remote(att_s.at[peer, s], att_ref.at[t, s], at_sem.at[d, s], at_rec.at[d, s], tp=peer)
            )
        own_at = pltpu.make_async_copy(att_s.at[t, s], att_ref.at[t, s], at_loc.at[s])
        own_at.start()
        at[0][s] = own_at
        if s == 0:
            line_step(4, 2)
            for k in range(3, T):
                line_step(3, k)
            every(relay, 3, every_p)
    prev_out = pltpu.make_async_copy(prev_s, prev_ref, out_sem.at[3])
    if far:
        prev_out.start()
    for k in range(3, T):
        line_step(4, k)
    every(take_chip, 2, every_p)
    keeps[2].wait()
    for tt in range(T):
        for ff in range(F):
            ow_ref[column(tt, hw), column(ff, shard)] = wo_s[tt, ff]
    every(relay, 4, every_p)
    for a in (3, 4):
        every(take_chip, a, every_p)
        keeps[a].wait()
    for s in range(S):
        at[0][s].wait()
        for d in range(1, T):
            at[d][s].wait_recv()
    normed_out.wait()
    for copy in outs:
        copy.wait()
    if far:
        prev_out.wait()
    for copy in pending:
        copy.wait_send()
    for a in range(5):
        drain(a)
    for s in range(S):
        for d in range(1, far + 1):
            @pl.when(c + d < C)
            def _():
                kv_copy(s, d).wait_send()


def front(start, low, wq, wo, wf, wp, params, block, far, counts):
    F, C, T = counts
    S, rows, width = start.shape
    hw = wq.shape[2]
    shard = wq.shape[1]
    heads = hw // HEAD_DIM
    hidden = wf.shape[1]
    bf, f32 = jnp.bfloat16, jnp.float32
    vmem = pl.BlockSpec(memory_space=pltpu.VMEM)
    anywhere = pl.BlockSpec(memory_space=pl.ANY)
    dma = lambda *shape: pltpu.SemaphoreType.DMA(shape)
    past = max(far, 1) * rows
    shape = jax.ShapeDtypeStruct
    return pl.pallas_call(
        functools.partial(front_kernel, counts, block),
        in_specs=[anywhere, vmem, anywhere, anywhere, anywhere, anywhere, anywhere],
        out_specs=[
            anywhere, anywhere, anywhere, anywhere, vmem, vmem, anywhere, anywhere, vmem, anywhere, anywhere, vmem
        ],
        out_shape=[
            shape((T, S, hw, rows // T), bf),
            shape((S, rows, hw), bf),
            shape((S, rows, 2 * hw), bf),
            shape((S, past, 2 * hw), bf),
            shape((S, hw, rows), f32),
            shape((S, 8, rows), f32),
            shape((S, rows, width), bf),
            shape((3, F * shard, hw), bf),
            shape((T * hw, F * shard), bf),
            shape((F * shard, T * hidden), bf),
            shape((F * shard, T * hidden), bf),
            shape((8, F * shard), f32),
        ],
        scratch_shapes=[
            pltpu.VMEM((S, rows, width), bf),
            pltpu.VMEM((S, rows, width), bf),
            pltpu.VMEM((3, F * shard, hw), bf),
            pltpu.VMEM((T, F, hw, shard), bf),
            pltpu.VMEM((F, 8, shard), f32),
            pltpu.VMEM((S, rows, hw), bf),
            pltpu.VMEM((S, rows, 2 * hw), bf),
            pltpu.VMEM((S, past, 2 * hw), bf),
            pltpu.VMEM((S, heads, HEAD_DIM, rows), bf),
            pltpu.VMEM((S, heads, rows, HEAD_DIM), bf),
            pltpu.VMEM((S, heads, HEAD_DIM, rows), bf),
            pltpu.VMEM((heads, past, HEAD_DIM), bf),
            pltpu.VMEM((heads, HEAD_DIM, past), bf),
            pltpu.VMEM((S, 8, rows), f32),
            pltpu.VMEM((S, 8, rows), f32),
            pltpu.VMEM((T, S, hw, rows // T), bf),
            dma(1), dma(5), dma(5),
            dma(5, 2 * T, 2), dma(5, 2 * T), dma(5, 2 * T), dma(5, 2 * T), dma(5, 2 * T), dma(5, 2 * T), dma(5, 2 * T),
            dma(5, 2 * T),
            dma(far + 1, S), dma(far + 1, S), dma(T, S), dma(T, S), dma(S),
        ],
        compiler_params=pltpu.CompilerParams(
            vmem_limit_bytes=VMEM_LIMIT, collective_id=1, has_side_effects=True
        ),
        cost_estimate=pl.CostEstimate(flops=8 * 10**9, bytes_accessed=64 << 20, transcendentals=8 << 20),
    )(start, low, wq, wo, wf, wp, params)


def padded(size):
    return -(-size // 128) * 128


def add_rows(target, sources, rows_at_once=16):
    def one(i, _):
        here = pl.ds(pl.multiple_of(i * rows_at_once, rows_at_once), rows_at_once)
        total = target[here, :].astype(jnp.float32)
        for source in sources:
            total = total + source[here, :].astype(jnp.float32)
        target[here, :] = total.astype(target.dtype)
        return 0

    lax.fori_loop(0, target.shape[0] // rows_at_once, one, 0)


def gelu_parts(x):
    square = x * x
    th = jnp.tanh(0.7978845608028654 * (x + 0.044715 * (square * x)))
    half = 0.5 * (1.0 + th)
    slope = half + (0.5 * x) * (1.0 - th * th) * (0.7978845608028654 * (1.0 + (3 * 0.044715) * square))
    return x * half, slope


def back_kernel(
    sizes, block, far, step_cols,
    att_ref, start_ref, grad_ref, outw_ref, fc_ref, pj_ref, params_ref,
    q_ref, kv_ref, prev_ref, low_ref, out_t_ref, log_ref, normed_ref, wl_ref, pick_ref,
    output_ref, dstart_ref, gw_ref, gq_ref, small_ref,
    start_s, mid_s, grad_s, ob_s, gbuf, rcore, rx, rc, rz, g2, r2c, r2x,
    da_s, da_r, dp_s, rec_s, kv_s, dq_s, rs_r, gq_s, rgq, rgc, sm_s, rst, rsc, rsf,
    in_sem, w_sem, core_sem, core_rec, x_sem, x_rec, c2_sem, c2_rec, x2_sem, x2_rec,
    c_sem, c_rec, z_sem, z_rec, b_sem, b_rec, da_sem, da_rec, dp_sem, dp_rec,
    rs_sem, rs_rec, ag_sem, ag_rec, gq_sem, gq_rec, gc_sem, gc_rec,
    st_sem, st_rec, sc_sem, sc_rec, sf_sem, sf_rec, loc_sem, wl_sem, credit,
):
    F, C, T = sizes
    f, c, t = lax.axis_index("fsdp"), lax.axis_index("ctx"), lax.axis_index("tp")
    S, rows, hw = q_ref.shape
    heads = hw // HEAD_DIM
    width = start_s.shape[2]
    own_rows = rows // T
    tokens = S * own_rows
    shard = gbuf.shape[1]
    hidden = fc_ref.shape[1] // T
    wide = 2 * hidden
    per_seq = rows // block
    bf, f32 = jnp.bfloat16, jnp.float32
    sib, across = f ^ 1, f ^ 2

    def remote(src, dst, send, recv, **where):
        return pltpu.make_async_remote_copy(
            src_ref=src, dst_ref=dst, send_sem=send, recv_sem=recv, device_id=where, device_id_type=MESH
        )

    pending = []

    def go(copy, like):
        copy.start()
        pending.append(like)

    def landed(ref, sem):
        remote(ref, ref, b_rec, sem, fsdp=f).wait_recv()

    def sent(ref, sem):
        remote(ref, ref, sem, b_rec, fsdp=f).wait_send()

    def tp_peer(d):
        return lax.rem(t + d, T)

    def tp_source(d):
        return lax.rem(t + T - d, T)

    def rows_of(owner):
        return pl.ds(pl.multiple_of(owner * own_rows, own_rows), own_rows)

    ag_own, ag_whole = (ob_s, ob_s), (output_ref, dstart_ref)

    def ag_copy(a, s, owner, step, way):
        whole = ag_whole[a].at[s, rows_of(owner), :]
        src = ag_own[a].at[s] if step == 0 else whole
        return lambda to: remote(src, whole, ag_sem.at[a, s, step, way], ag_rec.at[a, s, step, way], tp=to)

    def ag_keep(a, s):
        return pltpu.make_async_copy(ag_own[a].at[s], ag_whole[a].at[s, rows_of(t), :], loc_sem.at[a, s])

    def ag_start(a, s):
        @pl.when(t < T - 1)
        def _():
            ag_copy(a, s, t, 0, 0)(t + 1).start()

        @pl.when(t > 0)
        def _():
            ag_copy(a, s, t, 0, 1)(t - 1).start()

        ag_keep(a, s).start()

    def ag_step(a, s, step):
        @pl.when(t >= step)
        def _():
            ag_copy(a, s, t - step, step - 1, 0)(t).wait_recv()

        @pl.when((t >= step) & (t < T - 1))
        def _():
            ag_copy(a, s, t - step, step, 0)(t + 1).start()

        @pl.when(t + step <= T - 1)
        def _():
            ag_copy(a, s, t + step, step - 1, 1)(t).wait_recv()

        @pl.when((t + step <= T - 1) & (t > 0))
        def _():
            ag_copy(a, s, t + step, step, 1)(t - 1).start()

    def ag_drain(a, s, first):
        if not first:
            ag_keep(a, s).wait()
        for step in range(first, T - 1 if first or a else 1):
            @pl.when((t >= step) & (t < T - 1))
            def _():
                ag_copy(a, s, t - step, step, 0)(t + 1).wait_send()

            @pl.when((t + step <= T - 1) & (t > 0))
            def _():
                ag_copy(a, s, t + step, step, 1)(t - 1).wait_send()

    across_at = lambda b: T + b
    main = pl.ds(0, wide)

    def core_send(b):
        slot = b % 2
        if b >= 2:
            pl.semaphore_wait(credit, 1)
        for k in range(2):
            remote(
                gbuf.at[2 * T + 2 * slot + k, :, main], rcore.at[slot, k],
                core_sem.at[b, k], core_rec.at[b, k], fsdp=sib,
            ).start()

    def core_add(b):
        slot = b % 2
        landed(rcore.at[slot, 1], core_rec.at[b, 1])
        add_rows(gbuf.at[across_at(b), :, main], [rcore.at[slot, 1]])
        out = gbuf.at[across_at(b), :, main]
        go(
            remote(out, rx.at[b, :, main], x_sem.at[b], x_rec.at[b], fsdp=across),
            lambda: (rx.at[b, :, main], x_sem.at[b]),
        )
        landed(rcore.at[slot, 0], core_rec.at[b, 0])
        add_rows(gbuf.at[b, :, main], [rcore.at[slot, 0]])
        if b < T - 2:
            pl.semaphore_signal(credit, inc=1, device_id={"fsdp": sib}, device_id_type=MESH)

    held = [b // C for b in range(T)]

    def ctx_copy(b, d, to):
        return remote(gbuf.at[b], rc.at[held[b], d - 1], c_sem.at[b], c_rec.at[b, d], ctx=to)

    def cross_add(b):
        landed(rx.at[b, :, main], x_rec.at[b])
        add_rows(gbuf.at[b, :, main], [rx.at[b, :, main]])

    def ctx_send(b):
        owner = b % C
        for d in range(1, C):
            @pl.when(lax.rem(c + d, C) == owner)
            def _():
                ctx_copy(b, d, owner).start()

    def ctx_wait(b):
        @pl.when(c == b % C)
        def _():
            for d in range(1, C):
                ctx_copy(b, d, c).wait_recv()
            if C > 1:
                add_rows(gbuf.at[b], [rc.at[held[b], d - 1] for d in range(1, C)])

    def z_round(b, step):
        def hop(to, way):
            return remote(gbuf.at[b], rz.at[held[b], way], z_sem.at[b], z_rec.at[b, way], tp=to)

        def visit(way, before, here):
            @pl.when((c == b % C) & here)
            def _():
                if step:
                    hop(t, way).wait_recv()
                    add_rows(gbuf.at[b], [rz.at[held[b], way]])

                @pl.when(before)
                def _():
                    hop(t - 1 if way == 0 else t + 1, way).start()

        if T - 1 - step >= b and b < T - 1:
            visit(0, t > b, t == T - 1 - step)
        if step <= b and b > 0:
            visit(1, t < b, t == step)

    def feed_phase(att_s, outw_s, w_s, x_s, nm_s, nmt_s, gt_s, acc_s):
        steps = hidden // step_cols
        ring = w_s.shape[0]
        total_steps = 2 * T * steps

        def stream(n):
            at = pl.ds(pl.multiple_of(lax.rem(n, T * steps) * step_cols, step_cols), step_cols)
            slot = lax.rem(n, ring)
            return [
                pltpu.make_async_copy(ref.at[:, at], w_s.at[slot, k], w_sem.at[slot, k])
                for k, ref in enumerate((fc_ref, pj_ref))
            ]

        def take(n):
            for copy in stream(n):
                copy.wait()

            @pl.when(n + ring - 1 < total_steps)
            def _():
                for copy in stream(n + ring - 1):
                    copy.start()

            return lax.rem(n, ring)

        loads = [
            pltpu.make_async_copy(att_ref, dq_s, in_sem.at[0]),
            pltpu.make_async_copy(outw_ref, outw_s, in_sem.at[1]),
            pltpu.make_async_copy(start_ref, start_s, in_sem.at[2]),
            pltpu.make_async_copy(grad_ref, grad_s, in_sem.at[3]),
        ]
        for copy in loads:
            copy.start()
        for n in range(ring - 1):
            for copy in stream(n):
                copy.start()

        barrier = pltpu.get_barrier_semaphore()
        peers = 0
        for d in range(1, F):
            pl.semaphore_signal(barrier, inc=1, device_id={"fsdp": f ^ d}, device_id_type=MESH)
            peers += 1
        for d in range(1, T):
            pl.semaphore_signal(barrier, inc=1, device_id={"tp": tp_peer(d)}, device_id_type=MESH)
            peers += 1
        for d in range(1, C):
            pl.semaphore_signal(barrier, inc=1, device_id={"ctx": lax.rem(c + d, C)}, device_id_type=MESH)
            peers += 1
        pl.semaphore_wait(barrier, peers)

        for copy in loads:
            copy.wait()
        mid = start_s[...].reshape(tokens, width).astype(f32)
        for g in range(T):
            for s in range(S):
                att_s[g, column(s, own_rows), :] = turn(dq_s[g, s])
            mid = mid + dot(att_s[g], outw_s[column(g, hw), :])
        mid_s[...] = mid
        hat, _ = hat_rows(mid)
        nm = hat * params_ref[1:2] + params_ref[3:4]
        nm_s[...] = nm.astype(bf)
        nmt_s[...] = turn_back(nm)
        gt_s[...] = turn(grad_s[...])
        acc_s[...] = jnp.zeros_like(acc_s)

        def forward(j, _):
            slot = take(j)
            x = dot(nm_s[...], w_s[slot, 0])
            x_s[j] = x
            act, _ = gelu_parts(x)
            acc_s[...] += dot(act.astype(bf), w_s[slot, 1], ((1,), (1,)))
            return 0

        lax.fori_loop(0, T * steps, forward, 0)
        ob_s[...] = (mid_s[...] + acc_s[...]).astype(bf).reshape(S, own_rows, width)
        for s in range(S):
            ag_start(0, s)
        acc_s[...] = jnp.zeros_like(acc_s)

        for n in range(T):
            if n >= 2:
                for k in range(2):
                    sent(rcore.at[0, 0], core_sem.at[n - 2, k])
            slot = n % 2

            def backward(j, _):
                here = pl.ds(pl.multiple_of(j * step_cols, step_cols), step_cols)
                there = pl.ds(pl.multiple_of(hidden + j * step_cols, step_cols), step_cols)
                at_w = take(T * steps + n * steps + j)
                fc, proj = w_s[at_w, 0], w_s[at_w, 1]
                act, slope = gelu_parts(x_s[n * steps + j])
                act = act.astype(bf)
                d_exp = (slope * dot(grad_s[...], proj)).astype(bf)
                acc_s[...] += dot(d_exp, fc, ((1,), (1,)))
                d_fc = dot(nmt_s[...], d_exp).astype(bf)
                d_proj = dot(gt_s[...], act).astype(bf)
                for ff in range(F):
                    r = f ^ ff
                    odd, half = lax.rem(r, 2), r // 2
                    at = (1 - odd) * (half * T + n) + odd * (2 * T + 2 * slot + half)
                    gbuf[at, :, here] = d_fc[column(ff, shard)]
                    gbuf[at, :, there] = d_proj[column(ff, shard)]
                return 0

            lax.fori_loop(0, steps, backward, 0)
            core_send(n)
            if n:
                core_add(n - 1)

        mid = mid_s[...]
        hat, inv = hat_rows(mid)
        d_nm = acc_s[...]
        d_mid = grad_s[...].astype(f32) + norm_back(hat, inv, params_ref[1:2], d_nm)
        d_mid_t = turn_back(d_mid)
        for g in range(T):
            d_att = dot(outw_s[column(g, hw), :], d_mid_t).astype(bf)
            for s in range(S):
                da_s[g, s] = d_att[:, column(s, own_rows)]
        for s in range(S):
            for d in range(1, T):
                go(
                    remote(da_s.at[tp_peer(d), s], da_r.at[t, s], da_sem.at[d, s], da_rec.at[d, s], tp=tp_peer(d)),
                    lambda d=d, s=s: (da_s.at[0, s], da_sem.at[d, s]),
                )
        sm_s[...] = jnp.zeros_like(sm_s)
        sm_s[1:2, :] = jnp.sum(d_nm * hat, axis=0, keepdims=True)
        sm_s[3:4, :] = jnp.sum(d_nm, axis=0, keepdims=True)
        mid_s[...] = d_mid
        if g2.shape[3] > hw:
            g2[:, :, :, hw:] = jnp.zeros(g2.shape[:3] + (g2.shape[3] - hw,), bf)
        for g in range(T):
            d_out = dot(d_mid_t, att_s[g]).astype(bf)
            for ff in range(F):
                g2[f ^ ff, g, :, :hw] = d_out[column(ff, shard)]
        core_add(T - 1)

    bf_mem = lambda *shape: pltpu.VMEM(shape, bf)
    f32_mem = lambda *shape: pltpu.VMEM(shape, f32)
    pl.run_scoped(
        feed_phase,
        bf_mem(T, tokens, hw), bf_mem(T * hw, width), bf_mem(3, 2, width, step_cols),
        f32_mem(T * hidden // step_cols, tokens, step_cols),
        bf_mem(tokens, width), bf_mem(width, tokens), bf_mem(width, tokens), f32_mem(tokens, width),
    )

    for k in range(2):
        out = g2.at[1 + 2 * k]
        go(
            remote(out, r2c.at[k], c2_sem.at[k], c2_rec.at[k], fsdp=sib),
            lambda k=k: (r2c.at[k], c2_sem.at[k]),
        )

    def dp_copy(d, s):
        return remote(
            dp_s.at[far - d, s], rec_s.at[d - 1, s], dp_sem.at[d, s], dp_rec.at[d, s], ctx=lax.rem(c + C - d, C)
        )

    def sums_along(snd, wl_s):
        def kv_sum(s):
            for d in range(1, far + 1):
                @pl.when(c + d < C)
                def _():
                    dp_copy(d, s).wait_recv()
                    for g in range(T):
                        kv_s[g, s] = (kv_s[g, s].astype(f32) + rec_s[d - 1, s, g].astype(f32)).astype(bf)

        def partials(s):
            if s == 0:
                pltpu.make_async_copy(wl_ref, wl_s, wl_sem).wait()

            def one(o, _):
                total = dot(wl_s[0], dq_s[o, s])
                for j in (1, 2):
                    total = total + dot(wl_s[j], kv_s[o, s, column(j - 1, hw), :])
                snd[s, o] = total.astype(bf)
                return 0

            lax.fori_loop(0, T, one, 0)

        def rs_copy(s, o, way, at):
            to = at - 1 if way == 0 else at + 1
            slot = T if (to == o and way == 1) else o
            return remote(
                snd.at[s, o], rs_r.at[s, slot], rs_sem.at[s, o], rs_rec.at[s, o, way], tp=t - 1 if way == 0 else t + 1
            )

        def rs_slot(s, k):
            for at in range(T):
                for way, o, begins in ((0, k - (T - 1 - at), at == T - 1), (1, T - 1 + at - k, at == 0)):
                    if not (0 <= o <= at if way == 0 else at <= o <= T - 1):
                        continue

                    @pl.when(t == at)
                    def _():
                        if not begins:
                            landed(rs_r.at[s, T if (o == at and way == 1) else o], rs_rec.at[s, o, way])
                        if o != at:
                            if not begins:
                                add_rows(snd.at[s, o], [rs_r.at[s, o]], 128)
                            before = o - 1 if way == 0 else o + 1
                            if 0 <= before < T:
                                sent(snd.at[s, before], rs_sem.at[s, before])
                            rs_copy(s, o, way, at).start()

        return kv_sum, partials, rs_slot

    def attention_phase(
        snd, wl_s, q_s, kvo_s, prv_s, ot_s, k_h, kt_h, v_h, q_h, qt_h, g_h, gt_h, dqt_s, dk_s, dv_s, del_s
    ):
        kv_sum, partials, rs_slot = sums_along(snd, wl_s)

        def loads(s):
            return [
                pltpu.make_async_copy(ref.at[s], mem, in_sem.at[k])
                for k, (ref, mem) in enumerate(((q_ref, q_s), (kv_ref, kvo_s), (out_t_ref, ot_s), (prev_ref, prv_s)))
            ]

        for copy in loads(0):
            copy.start()
        for k in (1, 0):
            landed(r2c.at[k], c2_rec.at[k])
            for b in range(T):
                add_rows(g2.at[2 * k, b], [r2c.at[k, b]])
            if k:
                go(remote(g2.at[2], r2x, x2_sem, x2_rec, fsdp=across), lambda: (r2x, x2_sem))

        def keys(s):
            for h in range(heads):
                q = q_s[:, column(h)].astype(f32) * 0.125
                q_h[h] = q.astype(bf)
                qt_h[h] = turn_back(q)
                if far:
                    k = prv_s[:, column(h)]
                    k_h[h, : far * rows] = k
                    kt_h[h, :, : far * rows] = turn(k)
                    v_h[h, : far * rows] = prv_s[:, column(heads + h)]
                k = kvo_s[:, column(h)]
                k_h[h, far * rows :] = k
                kt_h[h, :, far * rows :] = turn(k)
                v_h[h, far * rows :] = kvo_s[:, column(heads + h)]

        def grads(s):
            da_r[t, s] = da_s[t, s]
            for d in range(1, T):
                landed(da_r.at[tp_source(d), s], da_rec.at[d, s])
            for h in range(heads):
                for g in range(T):
                    gt_h[h, :, column(g, own_rows)] = da_r[g, s, column(h), :]
                g_t = gt_h[h].astype(f32)
                g_h[h] = turn_back(g_t)
                del_s[h : h + 1, :] = jnp.sum(g_t * ot_s[column(h), :], axis=0, keepdims=True)
            dqt_s[...] = jnp.zeros_like(dqt_s)

        def part(s, h, base, count, own):
            spot = pl.ds(pl.multiple_of(h * HEAD_DIM, HEAD_DIM), HEAD_DIM)
            dk_s[:count] = jnp.zeros((count, HEAD_DIM), f32)
            dv_s[:count] = jnp.zeros((count, HEAD_DIM), f32)
            for i in range(per_seq):
                span = column(i, block)
                reach = far * rows + i * block
                first = max(0, reach - (DOC_MOST - 1) - base) // block * block
                last = min(count, reach + block - base)
                if first >= last:
                    continue
                low = low_ref[s, :, span] - base
                place = first + lax.broadcasted_iota(jnp.int32, (last - first, 1), 0)
                allowed = place >= low
                if own:
                    allowed = allowed & (place <= i * block + lax.broadcasted_iota(jnp.int32, (1, block), 1))
                here = slice(base + first, base + last)
                scores = dot(k_h[h, here, :], qt_h[h, :, span])
                p = jnp.exp(jnp.where(allowed, scores - log_ref[s, pl.ds(h, 1), span], MASKED))
                ds = (p * (dot(v_h[h, here, :], gt_h[h, :, span]) - del_s[pl.ds(h, 1), span])).astype(bf)
                dv_s[first:last] += dot(p.astype(bf), g_h[h, span, :])
                dk_s[first:last] += dot(ds, q_h[h, span, :])
                dqt_s[spot, span] += dot(kt_h[h, :, here], ds)
            return spot, pl.ds(pl.multiple_of(hw + h * HEAD_DIM, HEAD_DIM), HEAD_DIM)

        def far_part(s):
            def one(h, _):
                k_at, v_at = part(s, h, 0, far * rows, False)
                for at, source in ((k_at, dk_s), (v_at, dv_s)):
                    turned = source[: far * rows].T.astype(bf)
                    for j in range(far):
                        for g in range(T):
                            dp_s[j, s, g, at, :] = turned[:, column(j * T + g, own_rows)]
                return 0

            lax.fori_loop(0, heads, one, 0)

        def own_part(s):
            def one(h, _):
                k_at, v_at = part(s, h, far * rows, rows, True)
                for at, source in ((k_at, dk_s), (v_at, dv_s)):
                    turned = source[:rows].T.astype(bf)
                    for g in range(T):
                        kv_s[g, s, at, :] = turned[:, column(g, own_rows)]
                return 0

            lax.fori_loop(0, heads, one, 0)

        for s in range(S):
            for copy in loads(s):
                copy.wait()
            keys(s)
            grads(s)
            if s + 1 < S:
                for copy in loads(s + 1):
                    copy.start()
            if s == 0:
                for other in range(S):
                    ag_step(0, other, 1)
            if far:
                @pl.when(c > 0)
                def _():
                    far_part(s)

                for d in range(1, far + 1):
                    @pl.when(c >= d)
                    def _():
                        dp_copy(d, s).start()
            if s:
                rs_slot(s - 1, 1)
            else:
                cross_add(0)
            own_part(s)
            for g in range(T):
                dq_s[g, s] = (0.125 * dqt_s[:, column(g, own_rows)]).astype(bf)
            if s:
                rs_slot(s - 1, 2)
            if s < T - 2:
                for other in range(S):
                    ag_step(0, other, s + 2)
            if s + 1 < T:
                cross_add(s + 1)
            kv_sum(s)
            partials(s)
            rs_slot(s, 0)

    def last_phase(snd, wl_s, normed_s, gq_acc, tot_s):
        kv_sum, partials, rs_slot = sums_along(snd, wl_s)
        normed_in = pltpu.make_async_copy(normed_ref, normed_s, in_sem.at[0])
        normed_in.start()

        gain = params_ref[0:1]

        def norm_stage(s):
            tot_s[...] = snd[s, t].astype(f32)

            @pl.when(t < T - 1)
            def _():
                tot_s[...] += rs_r[s, t].astype(f32)

            @pl.when(t > 0)
            def _():
                tot_s[...] += rs_r[s, T].astype(f32)

            d_normed = tot_s[...].T
            hat, inv = hat_rows(start_s[s].astype(f32))
            value = mid_s[column(s, own_rows), :] + norm_back(hat, inv, gain, d_normed)
            ag_drain(0, s, 0)
            ob_s[s] = value.astype(bf)
            ag_start(1, s)
            sm_s[0:1, :] += jnp.sum(d_normed * hat, axis=0, keepdims=True)
            sm_s[2:3, :] += jnp.sum(d_normed, axis=0, keepdims=True)

        for k in range(3, T):
            rs_slot(0, k)
        norm_stage(0)
        landed(r2x, x2_rec)
        side = pl.ds(wide, g2.shape[3])
        for b in range(T):
            gbuf[b, :, side] = (g2[0, b].astype(f32) + r2x[b].astype(f32)).astype(bf)
        for b in range(min(S + 1, T)):
            ctx_send(b)

        normed_in.wait()
        gq_acc[...] = jnp.zeros_like(gq_acc)
        for s in range(S):

            def one(o, _):
                near = normed_s[s, rows_of(o), :]
                gq_acc[:hw, :] += dot(dq_s[o, s], near)
                gq_acc[hw:, :] += dot(kv_s[o, s], near)
                return 0

            lax.fori_loop(0, T, one, 0)
        for k in range(F):
            gq_s[k] = gq_acc[:, column(k, shard)].astype(bf)
        for d in range(1, F):
            go(
                remote(gq_s.at[f ^ d], rgq.at[d - 1], gq_sem.at[d], gq_rec.at[d], fsdp=f ^ d),
                lambda d=d: (gq_s.at[0], gq_sem.at[d]),
            )
        for b in range(min(S + 1, T), T):
            cross_add(b)
            ctx_send(b)
        for s in range(1, S):
            for k in range(1, T):
                rs_slot(s, k)
                if k == T - 2:
                    ag_step(1, 0, 1)
            norm_stage(s)

        thoughts = jnp.zeros((pick_ref.shape[1], width), f32)
        for s in range(S):
            thoughts = thoughts + dot(pick_ref[s], ob_s[s])
        sm_s[8:, :] = thoughts
        for d in range(1, T):
            go(
                remote(sm_s, rst.at[d], st_sem.at[d], st_rec.at[d], tp=tp_peer(d)),
                lambda d=d: (sm_s, st_sem.at[d]),
            )
        for b in range(T):
            ctx_wait(b)
            z_round(b, 0)

        gq_sum = gq_s[f].astype(f32)
        for d in range(1, F):
            landed(rgq.at[d - 1], gq_rec.at[d])
            gq_sum = gq_sum + rgq[d - 1].astype(f32)
        rgc[c] = gq_sum.astype(bf)
        for d in range(1, C):
            go(
                remote(rgc.at[c], rgc.at[c], gc_sem.at[d], gc_rec.at[d], ctx=lax.rem(c + d, C)),
                lambda d=d: (rgc.at[0], gc_sem.at[d]),
            )

        for d in range(1, T):
            landed(rst.at[d], st_rec.at[d])
        rst[0] = sm_s[...]
        total = jnp.zeros(sm_s.shape, f32)
        for k in range(T):
            total = total + rst[lax.rem(t + T - k, T)]
        rsc[c] = total
        for d in range(1, C):
            go(
                remote(rsc.at[c], rsc.at[c], sc_sem.at[d], sc_rec.at[d], ctx=lax.rem(c + d, C)),
                lambda d=d: (rsc.at[0], sc_sem.at[d]),
            )
        for step in range(1, T):
            if step > 1:
                ag_step(1, 0, step)
            for s in range(1, S):
                ag_step(1, s, step)
            for b in range(T):
                z_round(b, step)
            if step == 1:
                for d in range(1, C):
                    landed(rsc.at[0], sc_rec.at[d])
                total = jnp.zeros(sm_s.shape, f32)
                for k in range(C):
                    total = total + rsc[k]
                small_ref[8:, :] = total[8:]
                rsf[f] = total
                for d in range(1, F):
                    go(
                        remote(rsf.at[f], rsf.at[f], sf_sem.at[d], sf_rec.at[d], fsdp=f ^ d),
                        lambda d=d: (rsf.at[0], sf_sem.at[d]),
                    )
        for d in range(1, F):
            landed(rsf.at[0], sf_rec.at[d])
        norms = jnp.zeros((8, sm_s.shape[1]), f32)
        for k in range(F):
            norms = norms + rsf[k, 0:8, :]
        small_ref[0:8, :] = norms

        for d in range(1, C):
            landed(rgc.at[0], gc_rec.at[d])
        total = jnp.zeros(gq_ref.shape, f32)
        for k in range(C):
            total = total + rgc[k].astype(f32)
        gq_ref[...] = total
        for o in range(T):
            @pl.when((t == o + 1) | (t == o - 1))
            def _():
                for s in range(S):
                    sent(snd.at[s, o], rs_sem.at[s, o])

    def after_feed(snd, wl_s):
        wl_in = pltpu.make_async_copy(wl_ref, wl_s, wl_sem)
        wl_in.start()
        pl.run_scoped(
            functools.partial(attention_phase, snd, wl_s),
            bf_mem(rows, hw), bf_mem(rows, 2 * hw), bf_mem(max(far, 1) * rows, 2 * hw), f32_mem(hw, rows),
            bf_mem(heads, (far + 1) * rows, HEAD_DIM), bf_mem(heads, HEAD_DIM, (far + 1) * rows),
            bf_mem(heads, (far + 1) * rows, HEAD_DIM),
            bf_mem(heads, rows, HEAD_DIM), bf_mem(heads, HEAD_DIM, rows),
            bf_mem(heads, rows, HEAD_DIM), bf_mem(heads, HEAD_DIM, rows),
            f32_mem(hw, rows), f32_mem(max(far, 1) * rows, HEAD_DIM), f32_mem(max(far, 1) * rows, HEAD_DIM),
            f32_mem(8, rows),
        )
        pl.run_scoped(
            functools.partial(last_phase, snd, wl_s),
            bf_mem(S, rows, width), f32_mem(3 * hw, width), f32_mem(width, own_rows),
        )

    pl.run_scoped(after_feed, bf_mem(S, T, width, own_rows), bf_mem(3, width, hw))

    for b in range(T):
        owner = b % C
        final = lambda d: remote(gbuf.at[b], rx.at[b], b_sem.at[d], b_rec, ctx=lax.rem(owner + d, C))

        @pl.when((t == b) & (c == owner))
        def _():
            for d in range(1, C):
                final(d).start()
            gw_ref[...] = gbuf[b]
            for d in range(1, C):
                final(d).wait_send()

        if C > 1:
            @pl.when((t == b) & (c != owner))
            def _():
                final(1).wait_recv()
                gw_ref[...] = rx[b]

    for like in pending:
        sent(*like())
    for n in range(max(T - 2, 0), T):
        for k in range(2):
            sent(rcore.at[0, 0], core_sem.at[n, k])
    for b in range(T):
        owner = b % C
        if C > 1:
            @pl.when(c != owner)
            def _():
                ctx_copy(b, 1, owner).wait_send()

        @pl.when((c == owner) & (t != b))
        def _():
            remote(gbuf.at[b], rz.at[held[b], 0], z_sem.at[b], z_rec.at[b, 0], tp=t).wait_send()
    for s in range(S):
        for d in range(1, far + 1):
            @pl.when(c >= d)
            def _():
                dp_copy(d, s).wait_send()
        ag_drain(0, s, 1)
        ag_drain(1, s, 0)


def back(att, start, grad, out_w, fc, proj_t, params, q, kv, prev, low, out_t, logs, normed, wl, pick, block, far, counts):
    F, C, T = counts
    S, rows, hw = q.shape
    width = normed.shape[2]
    own_rows = rows // T
    tokens = S * own_rows
    shard = width // F
    hidden = fc.shape[1] // T
    cols = padded(hw)
    wide = 2 * hidden + cols
    bf, f32 = jnp.bfloat16, jnp.float32
    extra = 8 + pick.shape[1]
    mine = -(-T // C)
    dists = max(far, 1)
    vmem = pl.BlockSpec(memory_space=pltpu.VMEM)
    anywhere = pl.BlockSpec(memory_space=pl.ANY)
    dma = lambda *shape: pltpu.SemaphoreType.DMA(shape)
    one = pltpu.SemaphoreType.DMA
    shape = jax.ShapeDtypeStruct
    b16 = lambda *size: pltpu.VMEM(size, bf)
    b32 = lambda *size: pltpu.VMEM(size, f32)
    return pl.pallas_call(
        functools.partial(back_kernel, counts, block, far, 256),
        in_specs=[anywhere] * 6 + [vmem] + [anywhere] * 3 + [vmem, anywhere, vmem, anywhere, anywhere, vmem],
        out_specs=[anywhere, anywhere, vmem, vmem, vmem],
        out_shape=[
            shape((S, rows, width), bf),
            shape((S, rows, width), bf),
            shape((shard, wide), bf),
            shape((3 * hw, shard), f32),
            shape((extra, width), f32),
        ],
        scratch_shapes=[
            b16(S, own_rows, width), b32(tokens, width), b16(tokens, width), b16(S, own_rows, width),
            b16(2 * T + 4, shard, wide), b16(2, 2, shard, 2 * hidden), b16(T, shard, wide),
            b16(mine, max(C - 1, 1), shard, wide), b16(mine, 2, shard, wide),
            b16(4, T, shard, cols), b16(2, T, shard, cols), b16(T, shard, cols),
            b16(T, S, hw, own_rows), b16(T, S, hw, own_rows),
            b16(dists, S, T, 2 * hw, own_rows), b16(dists, S, T, 2 * hw, own_rows),
            b16(T, S, 2 * hw, own_rows), b16(T, S, hw, own_rows),
            b16(S, T + 1, width, own_rows),
            b16(F, 3 * hw, shard), b16(F - 1, 3 * hw, shard), b16(C, 3 * hw, shard),
            b32(extra, width), b32(T, extra, width), b32(C, extra, width), b32(F, extra, width),
            dma(4), dma(3, 2), dma(T, 2), dma(T, 2), dma(T), dma(T), dma(2), dma(2), one, one,
            dma(T), dma(T, C), dma(T), dma(T, 2), dma(C), one, dma(T, S), dma(T, S), dma(far + 1, S), dma(far + 1, S),
            dma(S, T), dma(S, T, 2), dma(2, S, T, 2), dma(2, S, T, 2), dma(F), dma(F), dma(C), dma(C),
            dma(T), dma(T), dma(C), dma(C), dma(F), dma(F), dma(2, S), one, pltpu.SemaphoreType.REGULAR,
        ],
        compiler_params=pltpu.CompilerParams(
            vmem_limit_bytes=VMEM_LIMIT, collective_id=2, has_side_effects=True
        ),
        cost_estimate=pl.CostEstimate(flops=36 * 10**9, bytes_accessed=100 << 20, transcendentals=16 << 20),
    )(att, start, grad, out_w, fc, proj_t, params, q, kv, prev, low, out_t, logs, normed, wl, pick)


def local(
    inputs, thoughts, positions, lengths, w_qkv, w_out, w_fc, w_proj, norm_gains, norm_biases, out_grad,
):
    rows, seqs, width = inputs.shape
    ctx_count = lax.axis_size("ctx")
    tp_count = lax.axis_size("tp")
    fsdp_count = lax.axis_size("fsdp")
    ctx, tp, fsdp = lax.axis_index("ctx"), lax.axis_index("tp"), lax.axis_index("fsdp")
    first_row = ctx * rows
    own_rows = rows // tp_count
    own_tokens = own_rows * seqs
    far = min(ctx_count - 1, -(-(DOC_MOST - 1) // rows))
    block = min(256, rows)
    bf, f32 = jnp.bfloat16, jnp.float32

    counts = (fsdp_count, ctx_count, tp_count)
    local_width = w_qkv.shape[2]
    params = jnp.pad(jnp.concatenate([norm_gains, norm_biases]).astype(f32), ((0, 4), (0, 0)))
    places = first_row + jnp.arange(rows, dtype=jnp.int32)
    is_thought = places[None, None, :] == positions[:, :, None]
    keep = jnp.logical_not(jnp.any(is_thought, axis=0))
    start = jnp.transpose(inputs, (1, 0, 2))
    for t in range(thoughts.shape[0]):
        start = jnp.where(is_thought[t][:, :, None], thoughts[t][:, None, :], start)
    ends = jnp.cumsum(lengths, axis=1, dtype=jnp.int32)
    low = jnp.max(jnp.where(ends[:, :, None] <= places[None, None, :], ends[:, :, None], 0), axis=1)
    low = low - (first_row - far * rows)

    low3 = low[:, None, :]
    attended, q, kv, prev, out_t, logs, normed, w_local, out_full, fc_full, proj_full_t, params = front(
        start, low3, w_qkv, w_out, w_fc, w_proj.T, params, block, far, counts
    )
    start_own = lax.dynamic_slice_in_dim(start, tp * own_rows, own_rows, 1)
    grad_own = jnp.transpose(
        lax.dynamic_slice_in_dim(out_grad, tp * own_rows, own_rows, 0), (1, 0, 2)
    ).reshape(own_tokens, width)

    own_places = lax.dynamic_slice_in_dim(places, tp * own_rows, own_rows, 0)
    count = thoughts.shape[0]
    pick = (own_places[None, None, :] == positions[:, :, None]).astype(bf)
    picks = []
    for s in range(seqs):
        picks.append(jnp.concatenate(
            [jnp.where(k == s, pick[:, s], jnp.zeros_like(pick[:, s])) for k in range(seqs)], axis=0
        ))
    pick = jnp.stack(picks)
    pick = jnp.pad(pick, ((0, 0), (0, -(-pick.shape[1] // 16) * 16 - pick.shape[1]), (0, 0)))
    output, d_start, gw, gq, small = back(
        attended, start_own, grad_own, out_full, fc_full, proj_full_t, params, q, kv, prev, low3, out_t, logs, normed,
        w_local, pick, block, far, counts,
    )
    output = jnp.transpose(output, (1, 0, 2))
    d_start = lax.optimization_barrier(jnp.transpose(d_start, (1, 0, 2)))
    d_inputs = jnp.where(keep.T[:, :, None], d_start.astype(f32), 0.0)
    d_thoughts = jnp.transpose(small[8 : 8 + count * seqs].reshape(seqs, count, width), (1, 0, 2))
    hidden = w_fc.shape[1]
    gw = gw.astype(f32)
    norms = lax.dynamic_slice_in_dim(small[:4], fsdp * w_fc.shape[0], w_fc.shape[0], 1)
    return (
        output,
        d_inputs,
        d_thoughts,
        jnp.transpose(gq.reshape(3, local_width, -1), (0, 2, 1)),
        gw[:, 2 * hidden : 2 * hidden + local_width].T,
        gw[:, :hidden],
        gw[:, hidden : 2 * hidden].T,
        norms[:2],
        norms[2],
        norms[3],
    )


def solution(mesh):
    in_specs = (
        P("ctx", "fsdp", None),
        P(None, "fsdp", None),
        P(None, "fsdp"),
        P("fsdp", None),
        P(None, "fsdp", "tp"),
        P("tp", "fsdp"),
        P("fsdp", "tp"),
        P("tp", "fsdp"),
        P(None, "fsdp"),
        P(None, "fsdp"),
        P("ctx", "fsdp", None),
    )
    out_specs = (
        P("ctx", "fsdp", None),
        P("ctx", "fsdp", None),
        P(None, "fsdp", None),
        P(None, "fsdp", "tp"),
        P("tp", "fsdp"),
        P("fsdp", "tp"),
        P("tp", "fsdp"),
        P(None, "fsdp"),
        P("fsdp"),
        P("fsdp"),
    )
    return jax.shard_map(local, mesh=mesh, in_specs=in_specs, out_specs=out_specs, check_vma=False)
```

profile of v0, /device:TPU:25, one launch (start us, length us, event | category | flops | bytes accessed | tf_op | source)
XLA Modules:
  0.0 358.4 jit_solution(10201321877376743387)
XLA Ops:
  0.7 0.8 copy.37
  1.4 0.1 fusion.13
  1.6 0.8 slice_bitcast_fusion.15
  2.4 0.0 copy-start.6
  2.4 0.0 copy-start.4
  2.4 0.0 copy-start.5
  2.4 8.6 %fusion.4.start_ref = bf16[2,1024,768]{2,1,0:T(8,128)(2,1)} fusion(bf16[1024,2,768]{2,1,0:T(2,128)(2,1)} %param.11, pred[2,1024]{1,0:T(4,128)(4,1)S(1)} %get-tuple-element.77, pred[2,1024]{1,0:T(4,128)(4,1)S(1)} %get-tuple-element.78, pred[2,1024]{1,0:T(4,128)(4,1)S(1)} %get-tuple-element.79, pred[2,1024]{1,0:T(4,128)(4,1)S(1)} %get-tuple-element.80, ...), kind=kLoop, calls=%fused_computation.6 | loop fusion | flops 9437184 | bytes 6322176 | tf_op jit(solution)/shard_map/jit(_where)/select_n | solution.py:1304
  11.0 0.0 copy-done.6
  11.0 0.2 reduce_window_sum.11
  11.2 0.1 copy.39
  11.3 0.1 fusion.7
  11.4 0.6 sub.22.low_ref
  12.0 0.6 fusion.12.par_ref
  12.6 91.4 %shard_map.186 = (bf16[4,2,192,256]{3,2,1,0:T(8,128)(2,1)}, bf16[2,1024,192]{2,1,0:T(8,128)(2,1)}, bf16[2,1024,384]{2,1,0:T(8,128)(2,1)}, bf16[2,1024,384]{2,1,0...) custom-call(bf16[2,1024,768]{2,1,0:T(8,128)(2,1)} %fusion.4.start_re, ...), custom_call_target="tpu_custom_call" | custom-call | flops 8000000000 | bytes 67108864 | tf_op jit(solution)/shard_map/pallas_call | solution.py:440
  104.0 2.1 constant_dynamic-slice_fusion.1.start_ref
  106.0 0.1 dynamic_slice.14
  106.1 0.1 compare_convert_fusion
  106.2 0.6 fusion.8.pick_ref
  106.8 1.7 dynamic-slice_bitcast_fusion
  108.5 1.0 copy.40
  109.5 226.4 %shard_map.187 = (bf16[2,1024,768]{2,1,0:T(8,128)(2,1)}, bf16[2,1024,768]{2,1,0:T(8,128)(2,1)}, bf16[192,1792]{1,0:T(8,128)(2,1)}, f32[576,192]{1,0:T(8,128)}, f32[24,768]{1,0:T(8,128)}) custom-call(bf16[4,2,192,256]{3,2,1,0:T(8,128)(2,1)} %get-tuple-element.27.att_ref, bf16[2,256,768]{2,1,0:T(8,128)(2,1)} %constant_dynamic-slice_fusion.1.start_ref, ...), custom_call_target="tpu_custom_call" | custom-call | flops 35999997952 | bytes 104857600 | tf_op jit(solution)/shard_map/pallas_call | solution.py:1247
  335.9 2.3 convert_select_fusion
  338.2 7.6 %copy.43 = f32[1024,2,768]{2,1,0:T(2,128)} copy(f32[1024,2,768]{2,0,1:T(8,128)S(1)} %convert_select_fusion) | data formatting | bytes 12582912
  345.8 6.9 %copy.42 = bf16[1024,2,768]{2,1,0:T(2,128)(2,1)} copy(bf16[1024,2,768]{2,0,1:T(8,128)(2,1)} %bitcast.61) | data formatting | bytes 6291456
  352.6 0.1 convert_element_type.16
  352.7 0.9 slice_bitcast_fusion
  353.6 0.8 copy.45
  354.4 1.1 copy.41
  355.5 0.9 slice.99
  356.3 0.6 copy.44
  357.0 0.6 fusion.14
  357.6 0.7 constant_dynamic-slice_fusion
  (20 shorter events, 0.1 us)
Async XLA Ops:
  2.4 8.6 %copy-start.6 = (s32[2,3]{1,0:T(2,128)S(1)}, s32[2,3]{1,0:T(2,128)}, u32[]{:S(2)}) copy-start(s32[2,3]{1,0:T(2,128)} %param.14) | copy-start | bytes 76
  2.4 9.6 %copy-start.4 = (bf16[2,192]{1,0:T(2,128)(2,1)S(1)}, bf16[2,192]{1,0:T(2,128)(2,1)}, u32[]{:S(2)}) copy-start(bf16[2,192]{1,0:T(2,128)(2,1)} %param.20) | copy-start | bytes 2308
  2.4 9.6 %copy-start.5 = (bf16[2,192]{1,0:T(2,128)(2,1)S(1)}, bf16[2,192]{1,0:T(2,128)(2,1)}, u32[]{:S(2)}) copy-start(bf16[2,192]{1,0:T(2,128)(2,1)} %param.19) | copy-start | bytes 2308
  12.6 93.5 %copy-start.3 = (s32[6,2]{0,1:T(2,128)S(1)}, s32[6,2]{0,1:T(2,128)}, u32[]{:S(2)}) copy-start(s32[6,2]{0,1:T(2,128)} %param.13) | copy-start | bytes 148
  345.8 6.9 %copy-start = (bf16[192,1792]{1,0:T(8,128)(2,1)S(1)}, bf16[192,1792]{1,0:T(8,128)(2,1)}, u32[]{:S(2)}) copy-start(bf16[192,1792]{1,0:T(8,128)(2,1)} %get-tuple-element.43) | copy-start | bytes 2064388
  352.6 1.8 copy-start.1
  352.6 3.7 %copy-start.2 = (f32[24,768]{1,0:T(8,128)S(1)}, f32[24,768]{1,0:T(8,128)}, u32[]{:S(2)}) copy-start(f32[24,768]{1,0:T(8,128)} %get-tuple-element.41) | copy-start | bytes 221188
where the time goes:
time: 365 us; the launch traced here: 358 us
  Pallas kernels  318 us (87%)
  local copies, waits for them, and re-layouts  27 us (7%)
  other arithmetic  12.7 us (3%)
    pallas_call x1, Pallas kernels, back(): pl.pallas_call(functools.partial(back_kernel, counts, block, far, 256), i...  226 us
    pallas_call x1, Pallas kernels, front(): pl.pallas_call(functools.partial(front_kernel, counts, block), in_specs=[...  91.4 us
    unnamed x19, local copies, waits for them, and re-layouts  16.6 us
    select_n x1, other arithmetic, local(): start = jnp.where(is_thought[t][:, :, None], thoughts[t][:, None, :], start)  8.59 us

commit v1 on v0

--- a/solution.py
+++ b/solution.py
@@ -349,11 +349,10 @@
         own_part(s)
         return 0
 
-    lax.fori_loop(0, 1, own_loop, 0)
+    lax.fori_loop(0, S, own_loop, 0)
     line_step(2, 2)
     line_step(4, 1)
     line_step(3, 2)
-    lax.fori_loop(1, S, own_loop, 0)
     for k in range(3, T):
         line_step(2, k)
     every(relay, 2, every_p)

time: 365 us -> 366 us (level)
  no operation moved by 1% of the time
where the time goes in v1:
time: 366 us; the launch traced here: 360 us
  Pallas kernels  320 us (87%)
  local copies, waits for them, and re-layouts  27 us (7%)
  other arithmetic  12.7 us (3%)
    pallas_call x1, Pallas kernels, back(): pl.pallas_call(functools.partial(back_kernel, counts, block, far, 256), i...  226 us
    pallas_call x1, Pallas kernels, front(): pl.pallas_call(functools.partial(front_kernel, counts, block), in_specs=[...  93.1 us
    unnamed x19, local copies, waits for them, and re-layouts  16.6 us
    select_n x1, other arithmetic, local(): start = jnp.where(is_thought[t][:, :, None], thoughts[t][:, None, :], start)  8.59 us

profile of v1, /device:TPU:25, one launch (start us, length us, event | category | flops | bytes accessed | tf_op | source)
XLA Modules:
  0.0 360.3 jit_solution(18443355329406334661)
XLA Ops:
  0.7 0.8 copy.37
  1.4 0.1 fusion.13
  1.6 0.8 slice_bitcast_fusion.15
  2.4 0.0 copy-start.6
  2.4 0.0 copy-start.4
  2.4 0.0 copy-start.5
  2.4 8.6 %fusion.4.start_ref = bf16[2,1024,768]{2,1,0:T(8,128)(2,1)} fusion(bf16[1024,2,768]{2,1,0:T(2,128)(2,1)} %param.11, pred[2,1024]{1,0:T(4,128)(4,1)S(1)} %get-tuple-element.77, pred[2,1024]{1,0:T(4,128)(4,1)S(1)} %get-tuple-element.78, pred[2,1024]{1,0:T(4,128)(4,1)S(1)} %get-tuple-element.79, pred[2,1024]{1,0:T(4,128)(4,1)S(1)} %get-tuple-element.80, ...), kind=kLoop, calls=%fused_computation.6 | loop fusion | flops 9437184 | bytes 6322176 | tf_op jit(solution)/shard_map/jit(_where)/select_n | solution.py:1303
  11.0 0.2 reduce_window_sum.11
  11.2 0.1 copy.39
  11.3 0.1 fusion.7
  11.4 0.6 sub.22.low_ref
  12.0 0.0 copy-done.5
  12.0 0.6 fusion.12.par_ref
  12.6 93.1 %shard_map.186 = (bf16[4,2,192,256]{3,2,1,0:T(8,128)(2,1)}, bf16[2,1024,192]{2,1,0:T(8,128)(2,1)}, bf16[2,1024,384]{2,1,0:T(8,128)(2,1)}, bf16[2,1024,384]{2,1,0...) custom-call(bf16[2,1024,768]{2,1,0:T(8,128)(2,1)} %fusion.4.start_re, ...), custom_call_target="tpu_custom_call" | custom-call | flops 8000000000 | bytes 67108864 | tf_op jit(solution)/shard_map/pallas_call | solution.py:439
  105.8 2.1 constant_dynamic-slice_fusion.1.start_ref
  107.8 0.1 dynamic_slice.14
  107.9 0.1 compare_convert_fusion
  108.0 0.6 fusion.8.pick_ref
  108.6 1.7 dynamic-slice_bitcast_fusion
  110.3 1.0 copy.40
  111.3 226.5 %shard_map.187 = (bf16[2,1024,768]{2,1,0:T(8,128)(2,1)}, bf16[2,1024,768]{2,1,0:T(8,128)(2,1)}, bf16[192,1792]{1,0:T(8,128)(2,1)}, f32[576,192]{1,0:T(8,128)}, f32[24,768]{1,0:T(8,128)}) custom-call(bf16[4,2,192,256]{3,2,1,0:T(8,128)(2,1)} %get-tuple-element.27.att_ref, bf16[2,256,768]{2,1,0:T(8,128)(2,1)} %constant_dynamic-slice_fusion.1.start_ref, ...), custom_call_target="tpu_custom_call" | custom-call | flops 35999997952 | bytes 104857600 | tf_op jit(solution)/shard_map/pallas_call | solution.py:1246
  337.7 2.3 convert_select_fusion
  340.0 7.6 %copy.43 = f32[1024,2,768]{2,1,0:T(2,128)} copy(f32[1024,2,768]{2,0,1:T(8,128)S(1)} %convert_select_fusion) | data formatting | bytes 12582912
  347.6 6.9 %copy.42 = bf16[1024,2,768]{2,1,0:T(2,128)(2,1)} copy(bf16[1024,2,768]{2,0,1:T(8,128)(2,1)} %bitcast.61) | data formatting | bytes 6291456
  354.4 0.1 convert_element_type.16
  354.5 0.9 slice_bitcast_fusion
  355.4 0.8 copy.45
  356.2 1.1 copy.41
  357.3 0.9 slice.99
  358.1 0.6 copy.44
  358.8 0.6 fusion.14
  359.4 0.7 constant_dynamic-slice_fusion
  (20 shorter events, 0.1 us)
Async XLA Ops:
  2.4 8.6 %copy-start.6 = (s32[2,3]{1,0:T(2,128)S(1)}, s32[2,3]{1,0:T(2,128)}, u32[]{:S(2)}) copy-start(s32[2,3]{1,0:T(2,128)} %param.14) | copy-start | bytes 76
  2.4 9.6 %copy-start.4 = (bf16[2,192]{1,0:T(2,128)(2,1)S(1)}, bf16[2,192]{1,0:T(2,128)(2,1)}, u32[]{:S(2)}) copy-start(bf16[2,192]{1,0:T(2,128)(2,1)} %param.20) | copy-start | bytes 2308
  2.4 9.6 %copy-start.5 = (bf16[2,192]{1,0:T(2,128)(2,1)S(1)}, bf16[2,192]{1,0:T(2,128)(2,1)}, u32[]{:S(2)}) copy-start(bf16[2,192]{1,0:T(2,128)(2,1)} %param.19) | copy-start | bytes 2308
  12.6 95.3 %copy-start.3 = (s32[6,2]{0,1:T(2,128)S(1)}, s32[6,2]{0,1:T(2,128)}, u32[]{:S(2)}) copy-start(s32[6,2]{0,1:T(2,128)} %param.13) | copy-start | bytes 148
  347.6 6.9 %copy-start = (bf16[192,1792]{1,0:T(8,128)(2,1)S(1)}, bf16[192,1792]{1,0:T(8,128)(2,1)}, u32[]{:S(2)}) copy-start(bf16[192,1792]{1,0:T(8,128)(2,1)} %get-tuple-element.43) | copy-start | bytes 2064388
  354.4 1.8 copy-start.1
  354.4 3.7 %copy-start.2 = (f32[24,768]{1,0:T(8,128)S(1)}, f32[24,768]{1,0:T(8,128)}, u32[]{:S(2)}) copy-start(f32[24,768]{1,0:T(8,128)} %get-tuple-element.41) | copy-start | bytes 221188
